TPU v7x, 512 devices: a whole 4x8x8 slice. The times are simulated.
512 devices in a mesh: vox: 32 (over x_lo, z, core), sta: 16 (over x_hi, y).
Axes of the slice: x: 4 (x_hi: 2, x_lo: 2; x = x_hi * 2 + x_lo), y: 8, z: 8, core: 2. Of those that a mesh axis runs over, the one named last changes fastest.
Arguments:
- green_tensor: bfloat16 [16, 6, 256, 4096], P('sta', None, None, 'vox'), may hold values from -0.078125 to 0.078125
- strain: bfloat16 [32, 6, 256, 4096], P('sta', None, None, 'vox'), may hold values from -6 to 6
- pair_events: int32 [16, 32], P('sta'), may hold values from -1 to 31, as said below
- pair_counts: int32 [16], P('sta'), may hold values from 22 to 32, as said below
- residuals: float32 [16, 32, 256], P('sta'), may hold values from -0.375 to 0.375
Outputs:
- kernel: float32 [4096], P(('vox', 'sta'))
Inputs may be any that keep to these rules, and one draw needn't show every extreme that they name: `pair_events`: within a station the live entries are distinct earthquakes; slots at or beyond the station's count hold -1. `pair_counts`: some station has exactly 32 live slots in every draw.
All inputs are finite; a program needn't handle non-finite values.
Results may differ from a plain program's by a relative error of at most 0.0029.
Values may be sent and summed in bfloat16 or wider, within the bound.
No kernel may reach another device: no remote copies, remote signals or barrier semaphores. Data moves between devices by JAX's collectives and lax.ppermute only.
A program may use at most 64 MiB of HBM per device.

v0:
```python
import jax
import jax.numpy as jnp
from jax import lax
from jax.sharding import PartitionSpec as P


def side_by_side(arrays, axis, dim, along):
    columns = [a.reshape(*a.shape[:along], -1) for a in arrays]
    both = jnp.concatenate(columns, axis=along)
    out, at, done = (lax.all_gather(both, axis, axis=dim, tiled=True), 0, [])
    for a, column in zip(arrays, columns):
        piece = out[..., at : at + column.shape[along]]
        done.append(piece.reshape(*piece.shape[:along], *a.shape[along:]))
        at += column.shape[along]
    return tuple(done)


def split_up(x, dim, count):
    before, after = (x.shape[:dim], x.shape[dim + 1 :])
    return jnp.moveaxis(x.reshape(*before, count, -1, *after), dim, 0)


def sum_at_owner(x, axis, dim):
    tiles = split_up(x, dim, lax.axis_size(axis))
    arrived = lax.all_to_all(tiles, axis, split_axis=0, concat_axis=0, tiled=True)
    return arrived.sum(axis=0)


def toeplitz(wave):
    length = wave.shape[-1]
    leading = wave.shape[:-1]
    padded = jnp.concatenate([jnp.zeros(leading + (length,), wave.dtype), wave], axis=-1)
    flipped = jnp.flip(padded, axis=-1)
    reps = (1,) * len(leading) + (length,)
    tiled = jnp.tile(flipped, reps)
    width = 2 * length - 1
    trimmed = tiled[..., : length * width]
    shaped = trimmed.reshape(leading + (length, width))
    return shaped[..., length - 1 :]


def contribution(block, strain, base):
    green, events, counts, resid = block
    local = base + jnp.arange(strain.shape[0], dtype=jnp.int32)
    live = jnp.arange(events.shape[1], dtype=jnp.int32)[None, :] < counts[:, None]
    match = ((events[:, :, None] == local[None, None, :]) & live[:, :, None]).astype(jnp.float32)
    combined = jnp.einsum("spe,spt->set", match, resid, precision=lax.Precision.HIGHEST)
    matrix = toeplitz(combined).astype(jnp.bfloat16)
    conv = jnp.einsum("setu,ecuv->sectv", matrix, strain, preferred_element_type=jnp.float32)
    return jnp.sum(conv * green[:, None].astype(jnp.float32), axis=(0, 1, 2, 3))


def body(green_tensor, strain, pair_events, pair_counts, residuals):
    base = lax.axis_index("sta") * strain.shape[0]
    block = (green_tensor, pair_events, pair_counts, residuals)
    kernel = contribution(
        (
            lax.all_gather(block[0], "sta", axis=0, tiled=True),
            *side_by_side((block[1], block[2]), "sta", 0, 1),
            lax.all_gather(block[3].astype(jnp.bfloat16), "sta", axis=0, tiled=True).astype(
                jnp.float32
            ),
        ),
        strain,
        base,
    )
    return sum_at_owner(kernel, "sta", 0)


def solution(mesh):
    in_specs = (
        P("sta", None, None, "vox"),
        P("sta", None, None, "vox"),
        P("sta", None),
        P("sta"),
        P("sta", None, None),
    )
    out_specs = P(("vox", "sta"))
    return jax.shard_map(body, mesh=mesh, in_specs=in_specs, out_specs=out_specs, check_vma=False)
```

profile of v0, /device:TPU:6, one launch (start us, length us, event | category | flops | bytes accessed | tf_op | source)
XLA Modules:
  0.0 171.9 jit_solution(8894927345608873170)
XLA Ops:
  6.5 0.0 copy-start
  6.5 0.0 all-gather.3.cloned.1.call-start
  6.5 0.7 all-gather.3.cloned.1.call-update
  7.9 0.8 convert_element_type.10
  8.7 0.7 add_bitcast_fusion
  9.4 39.6 %all-gather = s32[16,1,33]{2,1,0:T(1,128)S(1)} all-gather(s32[1,1,33]{2,1,0:T(1,128)S(1)} %add_bitcast_fusion), channel_id=1, replica_groups=mesh['vox'=32,'sta'=16] {'sta'}, dimensions={0}, use_global_device_ids=true | all-gather | bytes 2244 | tf_op jit(solution)/shard_map/all_gather | solution.py:10
  49.0 0.2 slice_reduce_fusion
  49.2 37.5 %all_gather.10 = bf16[16,32,256]{2,1,0:T(8,128)(2,1)S(1)} all-gather(bf16[1,32,256]{2,1,0:T(8,128)(2,1)S(1)} %convert_element_type.10), channel_id=1, replica_groups=mesh['vox'=32,'sta'=16] {'sta'}, dimensions={0}, use_global_device_ids=true | all-gather | bytes 278528 | tf_op jit(solution)/shard_map/all_gather | solution.py:60
  86.7 0.1 iota_compare_fusion
  86.8 0.2 fusion.2
  87.0 0.5 rev.4
  87.6 3.9 %tile.10 = bf16[16,2,256,512]{3,2,0,1:T(8,128)(2,1)} broadcast(bf16[16,2,512]{2,0,1:T(8,128)(2,1)S(1)} %copy.8), dimensions={0,1,3} | broadcast | bytes 8421376 | tf_op jit(solution)/shard_map/tile | solution.py:35
  91.4 8.9 %tile.11 = bf16[16,2,131072]{2,0,1:T(8,128)(2,1)} reshape(bf16[16,2,256,512]{3,2,0,1:T(8,128)(2,1)} %tile.10) | data formatting | bytes 16777216 | tf_op jit(solution)/shard_map/tile | solution.py:35
  100.3 7.2 %slice.23 = bf16[16,2,130816]{2,0,1:T(8,128)(2,1)} slice(bf16[16,2,131072]{2,0,1:T(8,128)(2,1)} %tile.11), slice={[0:16], [0:2], [0:130816]} | slice | bytes 16744448 | tf_op jit(solution)/shard_map/slice | solution.py:37
  107.5 19.5 %reshape.45 = bf16[16,2,256,511]{3,2,0,1:T(8,128)(2,1)} reshape(bf16[16,2,130816]{2,0,1:T(8,128)(2,1)} %slice.23) | data formatting | bytes 16744448 | tf_op jit(solution)/shard_map/reshape | solution.py:38
  127.0 7.8 %all-gather.3.cloned.1.call-done = bf16[16,6,256,128]{3,2,1,0:T(8,128)(2,1)} async-done(((bf16[1,6,256,128]{3,2,1,0:T(8,128)(2,1)}), bf16[16,6,256,128]{3,2,1,0:T(8,128)(2,1)}) %all-gather.3.cloned.1.call-update) | async-done | bytes 6291472 | tf_op jit(solution)/shard_map/all_gather | solution.py:58
  134.8 4.5 %convert_element_type.11 = f32[16,6,256,128]{3,2,1,0:T(8,128)S(1)} convert(bf16[16,6,256,128]{3,2,1,0:T(8,128)(2,1)} %all-gather.3.cloned.1.call-done) | non-fusion elementwise | flops 3145728 | bytes 18874368 | tf_op jit(solution)/shard_map/convert_element_type | solution.py:50
  139.3 0.0 copy-done
  139.3 10.7 %fusion = f32[128]{0:T(128)S(1)} fusion(f32[16,6,256,128]{3,2,1,0:T(8,128)S(1)} %convert_element_type.11, bf16[16,2,256,511]{3,2,0,1:T(8,128)(2,1)} %reshape.45, bf16[2,6,256,128]{3,2,1,0:T(8,128)(2,1)S(1)} %copy-done), kind=kOutput, calls=%fused_computation.1 | convolution fusion | flops 3233808384 | bytes 17564160 | tf_op jit(solution)/shard_map/setu,ecuv->sectv/dot_general | solution.py:49
  150.0 0.1 all_to_all.6
  150.1 14.4 %all_to_all.9 = f32[16,1,8]{2,1,0:T(1,128)S(1)} all-to-all(f32[16,1,8]{2,1,0:T(1,128)S(1)} %bitcast.30), channel_id=1, replica_groups=mesh['vox'=32,'sta'=16] {'sta'}, dimensions={0} | all-to-all | bytes 1024 | tf_op jit(solution)/shard_map/all_to_all | solution.py:25
  164.5 0.5 reduce_sum.19
  (3 shorter events, 0.0 us)
Async XLA Ops:
  6.5 132.8 %copy-start = (bf16[2,6,256,128]{3,2,1,0:T(8,128)(2,1)S(1)}, bf16[2,6,256,128]{3,2,1,0:T(8,128)(2,1)}, u32[]{:S(2)}) copy-start(bf16[2,6,256,128]{3,2,1,0:T(8,128)(2,1)} %param.6) | copy-start | bytes 2359300
  6.5 128.3 %all-gather.3.cloned.1.call-start = ((), (), s32[]{:S(2)}) async-start(), calls=%async_computation.1 | async-start | bytes 6684672 | tf_op jit(solution)/shard_map/all_gather | solution.py:58
Sparse Core Ops, SparseCore 0:
  10.5 124.2 all-gather.2
where the time goes:
time: 174 us; the launch traced here: 172 us
  blocking collectives  91.5 us (53%)
  local copies, waits for them, and re-layouts  40.2 us (23%)
  between operations  14.1 us (8%)
  matrix products  10.9 us (6%)
  waiting for transfers between devices  8.53 us (5%)
  other arithmetic  6.62 us (4%)
    all_gather x1, blocking collectives, side_by_side(): out, at, done = (lax.all_gather(both, axis, axis=dim, tiled=True), 0, [])  39.6 us
    all_gather x1, blocking collectives, body(): lax.all_gather(block[3].astype(jnp.bfloat16), 'sta', axis=0, tiled=True)  37.5 us
    reshape x1, local copies, waits for them, and re-layouts, toeplitz(): shaped = trimmed.reshape(leading + (length, width))  19.5 us
    all_to_all x1, blocking collectives, sum_at_owner(): lax.all_to_all(tiles, axis, split_axis=0, concat_axis=0, tiled=True)  14.4 us
    another operation x2, local copies, waits for them, and re-layouts, toeplitz(): tiled = jnp.tile(flipped, reps)  12.8 us
    dot_general x1, matrix products, contribution(): jnp.einsum('setu,ecuv->sectv', matrix, strain, preferred_element_type=jnp...  10.7 us
    all_gather x1, waiting for transfers between devices, body(): lax.all_gather(block[0], 'sta', axis=0, tiled=True)  7.82 us
    slice x1, local copies, waits for them, and re-layouts, toeplitz(): trimmed = tiled[..., :length * width]  7.16 us
  transfers between devices with their start and end apart: 1, of which 1 were waited for; matrix products, arithmetic and copies ran while one was open for 24% of the time, Pallas kernels for 0%

commit v1 on v0

v1 whole, which is shorter than its diff:
```python
import jax
import jax.numpy as jnp
from jax import lax
from jax.experimental import pallas as pl
from jax.experimental.pallas import tpu as pltpu
from jax.sharding import PartitionSpec as P

COMP = 6
NT = 256
STA = 16
MAXP = 32
EVENTS = 32
OWN = 8
LAG = 32
BLOCKS = NT // LAG
S_COLS = COMP * 2 * NT
G_AT = S_COLS
R_AT = G_AT + COMP * NT
COLS = R_AT + (EVENTS // 8) * NT
F32 = jnp.float32
BF16 = jnp.bfloat16


def pack_kernel(counts_ref, green_ref, strain_ref, events_ref, resid_ref, out_ref):
    voxels = green_ref.shape[-1]
    for c in range(COMP):
        for half in range(2):
            rows = []
            for j in range(half * BLOCKS // 2, (half + 1) * BLOCKS // 2):
                for e in range(2):
                    rows.append(strain_ref[e, c, LAG * j : LAG * (j + 1), :])
            block = jnp.concatenate(rows, axis=0)
            at = c * 2 * NT + half * NT
            out_ref[:, at : at + NT] = block.T
        at = G_AT + c * NT
        out_ref[:, at : at + NT] = green_ref[0, c].T
    wave = resid_ref[0].astype(BF16)
    row = lax.broadcasted_iota(jnp.int32, (voxels, MAXP), 0)
    slot = lax.broadcasted_iota(jnp.int32, (voxels, MAXP), 1)
    paired = jnp.broadcast_to(events_ref[...], (voxels, MAXP))
    for m in range(EVENTS // 8):
        match = (paired == 8 * m + row % 8) & (slot < counts_ref[0])
        picked = jnp.dot(match.astype(F32).astype(BF16), wave, preferred_element_type=F32)
        out_ref[:, R_AT + m * NT : R_AT + (m + 1) * NT] = picked.astype(BF16)


def pack(green, strain, events, counts, resid):
    voxels = green.shape[-1]
    vmem = pl.BlockSpec(memory_space=pltpu.VMEM)
    return pl.pallas_call(
        pack_kernel,
        out_shape=jax.ShapeDtypeStruct((voxels, COLS), BF16),
        in_specs=[pl.BlockSpec(memory_space=pltpu.SMEM), vmem, vmem, vmem, vmem],
        out_specs=vmem,
        compiler_params=pltpu.CompilerParams(vmem_limit_bytes=32 << 20),
        name="pack",
    )(counts, green, strain, events, resid)


def product_kernel(y_ref, out_ref, x_ref, w_ref, acc_ref):
    lane = lax.broadcasted_iota(jnp.int32, (8, 128), 1)
    low = lane < 64
    for at in range(STA // 2):
        for jj in range(BLOCKS // 2):
            for cc in range(COMP // 2):
                first, second = ([], [])
                for c in (2 * cc, 2 * cc + 1):
                    col = c * 2 * NT + jj * 128
                    a = y_ref[2 * at, :, col : col + 128].astype(F32)
                    b = y_ref[2 * at + 1, :, col : col + 128].astype(F32)
                    crossed = pltpu.roll(jnp.where(low, b, a), 64, 1)
                    first.append(jnp.where(low, a, crossed))
                    second.append(jnp.where(low, crossed, b))
                for j, pair in ((2 * jj, first), (2 * jj + 1, second)):
                    r = (j * COMP + 2 * cc) * OWN
                    x_ref[r : r + 16, at * 128 : at * 128 + 128] = jnp.concatenate(pair, axis=0).astype(BF16)

    upper = lax.broadcasted_iota(jnp.int32, (LAG, NT), 1) >= lax.broadcasted_iota(jnp.int32, (LAG, NT), 0)
    wide = lax.broadcasted_iota(jnp.int32, (COMP * OWN, NT), 1)

    def build(s, slot):
        for m in range(EVENTS // 8):
            waves = y_ref[s, :, R_AT + m * NT : R_AT + (m + 1) * NT].astype(F32)
            for q in range(8):
                wave = jnp.broadcast_to(waves[q : q + 1, :], (LAG, NT))
                shifted = pltpu.roll(wave, 0, 1, stride=1, stride_axis=0)
                at = (8 * m + q) * LAG
                w_ref[slot, at : at + LAG, :] = jnp.where(upper, shifted, 0.0).astype(BF16)

    build(0, 0)
    acc_ref[...] = jnp.zeros_like(acc_ref)

    def step(s, carry):
        slot = lax.rem(s, 2)
        build(jnp.minimum(s + 1, STA - 1), 1 - slot)
        half = COMP * OWN * BLOCKS // 2
        near = jnp.dot(x_ref[:half, :], w_ref[slot], preferred_element_type=F32)
        far = jnp.dot(x_ref[half:, :], w_ref[slot, :, :128], preferred_element_type=F32)
        green = jnp.concatenate(
            [y_ref[s, :, G_AT + c * NT : G_AT + (c + 1) * NT].astype(F32) for c in range(COMP)], axis=0
        )
        total = acc_ref[...]
        for j in range(BLOCKS // 2):
            later = green
            if j:
                later = jnp.where(wide < NT - LAG * j, pltpu.roll(green, NT - LAG * j, 1), 0.0)
            rows = slice(j * COMP * OWN, (j + 1) * COMP * OWN)
            terms = near[rows] * later
            terms = terms[:, :128] + terms[:, 128:] + far[rows] * later[:, 128:]
            for c in range(COMP):
                total = total + terms[c * OWN : (c + 1) * OWN]
        acc_ref[...] = total
        return carry

    lax.fori_loop(0, STA, step, 0)
    sums = jnp.sum(acc_ref[...], axis=1, keepdims=True)
    row = lax.broadcasted_iota(jnp.int32, (8, 128), 0)
    spread = jnp.sum(jnp.where(row == lane, sums, 0.0), axis=0, keepdims=True)
    out_ref[...] = spread[:, :OWN]


def product(arrived):
    vmem = pl.BlockSpec(memory_space=pltpu.VMEM)
    width = COMP * OWN * BLOCKS
    return pl.pallas_call(
        product_kernel,
        out_shape=jax.ShapeDtypeStruct((1, OWN), F32),
        in_specs=[vmem],
        out_specs=vmem,
        scratch_shapes=[
            pltpu.VMEM((width, EVENTS * LAG), BF16),
            pltpu.VMEM((2, EVENTS * LAG, NT), BF16),
            pltpu.VMEM((OWN, 128), F32),
        ],
        compiler_params=pltpu.CompilerParams(vmem_limit_bytes=32 << 20),
        name="product",
    )(arrived)


def body(green_tensor, strain, pair_events, pair_counts, residuals):
    packed = pack(green_tensor, strain, pair_events, pair_counts, residuals)
    tiles = packed.reshape(STA, OWN, COLS)
    arrived = lax.all_to_all(tiles, "sta", split_axis=0, concat_axis=0, tiled=True)
    return product(arrived).reshape(OWN)


def solution(mesh):
    in_specs = (
        P("sta", None, None, "vox"),
        P("sta", None, None, "vox"),
        P("sta", None),
        P("sta"),
        P("sta", None, None),
    )
    out_specs = P(("vox", "sta"))
    return jax.shard_map(body, mesh=mesh, in_specs=in_specs, out_specs=out_specs, check_vma=False)
```

time: 174 us -> 62.7 us (0.36)
  the two profiles are of different devices: /device:TPU:6 before, /device:TPU:392 now
where the time goes in v1:
time: 62.7 us; the launch traced here: 62.5 us
  blocking collectives  46.4 us (74%)
  Pallas kernels  11.8 us (19%)
  local copies, waits for them, and re-layouts  3.53 us (6%)
  between operations  0.67 us (1%)
    all_to_all x1, blocking collectives, body(): lax.all_to_all(tiles, 'sta', split_axis=0, concat_axis=0, tiled=True)  46.4 us
    pallas_call x1, Pallas kernels, product(): pl.pallas_call(product_kernel, out_shape=jax.ShapeDtypeStruct((1, OWN), F...  11.4 us
    unnamed x8, local copies, waits for them, and re-layouts  3.53 us

profile of v1, /device:TPU:392, one launch (start us, length us, event | category | flops | bytes accessed | tf_op | source)
XLA Modules:
  0.0 62.5 jit_solution(11945681653067255878)
XLA Ops:
  0.7 0.0 copy-start
  0.7 1.1 %copy-done = bf16[2,6,256,128]{3,2,1,0:T(8,128)(2,1)S(1)} copy-done((bf16[2,6,256,128]{3,2,1,0:T(8,128)(2,1)S(1)}, bf16[2,6,256,128]{3,2,1,0:T(8,128)(2,1)}, u32[]{:S(2)}) %copy-start) | copy-done | bytes 786456
  1.8 0.0 copy-start.1
  1.8 1.0 %copy-done.1 = bf16[1,6,256,128]{3,2,1,0:T(8,128)(2,1)S(1)} copy-done((bf16[1,6,256,128]{3,2,1,0:T(8,128)(2,1)S(1)}, bf16[1,6,256,128]{3,2,1,0:T(8,128)(2,1)}, u32[]{:S(2)}) %copy-start.1) | copy-done | bytes 393240
  2.8 0.0 copy-start.2
  2.8 0.8 %copy-done.2 = f32[1,32,256]{2,1,0:T(8,128)S(1)} copy-done((f32[1,32,256]{2,1,0:T(8,128)S(1)}, f32[1,32,256]{2,1,0:T(8,128)}, u32[]{:S(2)}) %copy-start.2) | copy-done | bytes 32792
  3.5 0.0 copy-start.3
  3.5 0.7 %copy-done.3 = s32[1,32]{1,0:T(1,128)S(1)} copy-done((s32[1,32]{1,0:T(1,128)S(1)}, s32[1,32]{1,0:T(1,128)}, u32[]{:S(2)}) %copy-start.3) | copy-done | bytes 152
  4.2 0.4 pack.1
  4.6 46.4 %all_to_all.5.y_ref = bf16[16,8,5632]{2,1,0:T(8,128)(2,1)S(1)} all-to-all(bf16[16,8,5632]{2,1,0:T(8,128)(2,1)S(1)} %bitcast.2), channel_id=1, replica_groups=mesh['vox'=32,'sta'=16] {'sta'}, dimensions={0} | all-to-all | bytes 2883584 | tf_op jit(solution)/shard_map/all_to_all | solution.py:143
  51.0 11.4 %product.1 = f32[1,8]{1,0:T(1,128)} custom-call(bf16[16,8,5632]{2,1,0:T(8,128)(2,1)S(1)} %all_to_all.5.y_ref), custom_call_target="tpu_custom_call" | custom-call | tf_op jit(solution)/shard_map/product/pallas_call | solution.py:125
Async XLA Ops:
  0.7 1.1 %copy-start = (bf16[2,6,256,128]{3,2,1,0:T(8,128)(2,1)S(1)}, bf16[2,6,256,128]{3,2,1,0:T(8,128)(2,1)}, u32[]{:S(2)}) copy-start(bf16[2,6,256,128]{3,2,1,0:T(8,128)(2,1)} %strain_ref.1) | copy-start | bytes 2359300
  1.8 1.0 %copy-start.1 = (bf16[1,6,256,128]{3,2,1,0:T(8,128)(2,1)S(1)}, bf16[1,6,256,128]{3,2,1,0:T(8,128)(2,1)}, u32[]{:S(2)}) copy-start(bf16[1,6,256,128]{3,2,1,0:T(8,128)(2,1)} %green_ref.1) | copy-start | bytes 1179652
  2.8 0.8 %copy-start.2 = (f32[1,32,256]{2,1,0:T(8,128)S(1)}, f32[1,32,256]{2,1,0:T(8,128)}, u32[]{:S(2)}) copy-start(f32[1,32,256]{2,1,0:T(8,128)} %resid_ref.1) | copy-start | bytes 98308
  3.5 0.7 %copy-start.3 = (s32[1,32]{1,0:T(1,128)S(1)}, s32[1,32]{1,0:T(1,128)}, u32[]{:S(2)}) copy-start(s32[1,32]{1,0:T(1,128)} %events_ref.1) | copy-start | bytes 388

commit v2 on v1

--- a/solution.py
+++ b/solution.py
@@ -21,9 +21,39 @@
 BF16 = jnp.bfloat16
 
 
-def pack_kernel(counts_ref, green_ref, strain_ref, events_ref, resid_ref, out_ref):
+def pack_kernel(
+    counts_hbm, green_hbm, strain_hbm, events_hbm, resid_hbm, out_ref,
+    count_ref, green_ref, strain_ref, events_ref, resid_ref, small_sem, green_sem, strain_sem,
+):
+    small = [
+        pltpu.make_async_copy(counts_hbm, count_ref, small_sem.at[0]),
+        pltpu.make_async_copy(events_hbm, events_ref, small_sem.at[1]),
+        pltpu.make_async_copy(resid_hbm, resid_ref, small_sem.at[2]),
+    ]
+    greens = [
+        pltpu.make_async_copy(green_hbm.at[:, c], green_ref.at[:, c], green_sem.at[c]) for c in range(COMP)
+    ]
+    strains = [
+        pltpu.make_async_copy(strain_hbm.at[:, c], strain_ref.at[:, c], strain_sem.at[c]) for c in range(COMP)
+    ]
+    for copy in small:
+        copy.start()
+    for c in range(COMP):
+        strains[c].start()
+        greens[c].start()
+    for copy in small:
+        copy.wait()
     voxels = green_ref.shape[-1]
+    wave = resid_ref[0].astype(BF16)
+    row = lax.broadcasted_iota(jnp.int32, (voxels, MAXP), 0)
+    slot = lax.broadcasted_iota(jnp.int32, (voxels, MAXP), 1)
+    paired = jnp.broadcast_to(events_ref[...], (voxels, MAXP))
+    for m in range(EVENTS // 8):
+        match = (paired == 8 * m + row % 8) & (slot < count_ref[0])
+        picked = jnp.dot(match.astype(F32).astype(BF16), wave, preferred_element_type=F32)
+        out_ref[:, R_AT + m * NT : R_AT + (m + 1) * NT] = picked.astype(BF16)
     for c in range(COMP):
+        strains[c].wait()
         for half in range(2):
             rows = []
             for j in range(half * BLOCKS // 2, (half + 1) * BLOCKS // 2):
@@ -32,32 +62,35 @@
             block = jnp.concatenate(rows, axis=0)
             at = c * 2 * NT + half * NT
             out_ref[:, at : at + NT] = block.T
+        greens[c].wait()
         at = G_AT + c * NT
         out_ref[:, at : at + NT] = green_ref[0, c].T
-    wave = resid_ref[0].astype(BF16)
-    row = lax.broadcasted_iota(jnp.int32, (voxels, MAXP), 0)
-    slot = lax.broadcasted_iota(jnp.int32, (voxels, MAXP), 1)
-    paired = jnp.broadcast_to(events_ref[...], (voxels, MAXP))
-    for m in range(EVENTS // 8):
-        match = (paired == 8 * m + row % 8) & (slot < counts_ref[0])
-        picked = jnp.dot(match.astype(F32).astype(BF16), wave, preferred_element_type=F32)
-        out_ref[:, R_AT + m * NT : R_AT + (m + 1) * NT] = picked.astype(BF16)
 
 
 def pack(green, strain, events, counts, resid):
     voxels = green.shape[-1]
-    vmem = pl.BlockSpec(memory_space=pltpu.VMEM)
+    whole = pl.BlockSpec(memory_space=pltpu.HBM)
     return pl.pallas_call(
         pack_kernel,
         out_shape=jax.ShapeDtypeStruct((voxels, COLS), BF16),
-        in_specs=[pl.BlockSpec(memory_space=pltpu.SMEM), vmem, vmem, vmem, vmem],
-        out_specs=vmem,
-        compiler_params=pltpu.CompilerParams(vmem_limit_bytes=32 << 20),
+        in_specs=[whole] * 5,
+        out_specs=pl.BlockSpec(memory_space=pltpu.VMEM),
+        scratch_shapes=[
+            pltpu.SMEM(counts.shape, counts.dtype),
+            pltpu.VMEM(green.shape, green.dtype),
+            pltpu.VMEM(strain.shape, strain.dtype),
+            pltpu.VMEM(events.shape, events.dtype),
+            pltpu.VMEM(resid.shape, resid.dtype),
+            pltpu.SemaphoreType.DMA((3,)),
+            pltpu.SemaphoreType.DMA((COMP,)),
+            pltpu.SemaphoreType.DMA((COMP,)),
+        ],
+        compiler_params=pltpu.CompilerParams(vmem_limit_bytes=48 << 20),
         name="pack",
-    )(counts, green, strain, events, resid)
+    )(counts, *[pltpu.with_memory_space_constraint(a, pltpu.HBM) for a in (green, strain, events, resid)])
 
 
-def product_kernel(y_ref, out_ref, x_ref, w_ref, acc_ref):
+def product_kernel(y_ref, out_ref, x_ref, *w_refs):
     lane = lax.broadcasted_iota(jnp.int32, (8, 128), 1)
     low = lane < 64
     for at in range(STA // 2):
@@ -78,42 +111,40 @@
     upper = lax.broadcasted_iota(jnp.int32, (LAG, NT), 1) >= lax.broadcasted_iota(jnp.int32, (LAG, NT), 0)
     wide = lax.broadcasted_iota(jnp.int32, (COMP * OWN, NT), 1)
 
-    def build(s, slot):
+    def build(s, w_ref):
         for m in range(EVENTS // 8):
             waves = y_ref[s, :, R_AT + m * NT : R_AT + (m + 1) * NT].astype(F32)
             for q in range(8):
                 wave = jnp.broadcast_to(waves[q : q + 1, :], (LAG, NT))
                 shifted = pltpu.roll(wave, 0, 1, stride=1, stride_axis=0)
                 at = (8 * m + q) * LAG
-                w_ref[slot, at : at + LAG, :] = jnp.where(upper, shifted, 0.0).astype(BF16)
+                w_ref[at : at + LAG, :] = jnp.where(upper, shifted, 0.0).astype(BF16)
 
-    build(0, 0)
-    acc_ref[...] = jnp.zeros_like(acc_ref)
-
-    def step(s, carry):
-        slot = lax.rem(s, 2)
-        build(jnp.minimum(s + 1, STA - 1), 1 - slot)
+    def station(s, w_ref, total):
         half = COMP * OWN * BLOCKS // 2
-        near = jnp.dot(x_ref[:half, :], w_ref[slot], preferred_element_type=F32)
-        far = jnp.dot(x_ref[half:, :], w_ref[slot, :, :128], preferred_element_type=F32)
+        both = jnp.dot(x_ref[...], w_ref[...], preferred_element_type=F32)
         green = jnp.concatenate(
             [y_ref[s, :, G_AT + c * NT : G_AT + (c + 1) * NT].astype(F32) for c in range(COMP)], axis=0
         )
-        total = acc_ref[...]
         for j in range(BLOCKS // 2):
             later = green
             if j:
                 later = jnp.where(wide < NT - LAG * j, pltpu.roll(green, NT - LAG * j, 1), 0.0)
-            rows = slice(j * COMP * OWN, (j + 1) * COMP * OWN)
-            terms = near[rows] * later
-            terms = terms[:, :128] + terms[:, 128:] + far[rows] * later[:, 128:]
+            near = both[j * COMP * OWN : (j + 1) * COMP * OWN]
+            far = both[half + j * COMP * OWN : half + (j + 1) * COMP * OWN, :128]
+            terms = near * later
+            terms = terms[:, :128] + terms[:, 128:] + far * later[:, 128:]
             for c in range(COMP):
                 total = total + terms[c * OWN : (c + 1) * OWN]
-        acc_ref[...] = total
-        return carry
+        return total
 
-    lax.fori_loop(0, STA, step, 0)
-    sums = jnp.sum(acc_ref[...], axis=1, keepdims=True)
+    total = jnp.zeros((OWN, 128), F32)
+    build(0, w_refs[0])
+    for s in range(STA):
+        if s + 1 < STA:
+            build(s + 1, w_refs[(s + 1) % 2])
+        total = station(s, w_refs[s % 2], total)
+    sums = jnp.sum(total, axis=1, keepdims=True)
     row = lax.broadcasted_iota(jnp.int32, (8, 128), 0)
     spread = jnp.sum(jnp.where(row == lane, sums, 0.0), axis=0, keepdims=True)
     out_ref[...] = spread[:, :OWN]
@@ -129,8 +160,8 @@
         out_specs=vmem,
         scratch_shapes=[
             pltpu.VMEM((width, EVENTS * LAG), BF16),
-            pltpu.VMEM((2, EVENTS * LAG, NT), BF16),
-            pltpu.VMEM((OWN, 128), F32),
+            pltpu.VMEM((EVENTS * LAG, NT), BF16),
+            pltpu.VMEM((EVENTS * LAG, NT), BF16),
         ],
         compiler_params=pltpu.CompilerParams(vmem_limit_bytes=32 << 20),
         name="product",

time: 62.7 us -> 54.2 us (0.86)
  the two profiles are of different devices: /device:TPU:392 before, /device:TPU:72 now
where the time goes in v2:
time: 54.2 us; the launch traced here: 54.1 us
  blocking collectives  46.4 us (86%)
  Pallas kernels  7.01 us (13%)
  between operations  0.66 us (1%)
    all_to_all x1, blocking collectives, body(): lax.all_to_all(tiles, 'sta', split_axis=0, concat_axis=0, tiled=True)  46.4 us
    pallas_call x1, Pallas kernels, product(): pl.pallas_call(product_kernel, out_shape=jax.ShapeDtypeStruct((1, OWN), F...  4.55 us
    pallas_call x1, Pallas kernels, pack(): pl.pallas_call(pack_kernel, out_shape=jax.ShapeDtypeStruct((voxels, COLS)...  2.45 us

profile of v2, /device:TPU:72, one launch (start us, length us, event | category | flops | bytes accessed | tf_op | source)
XLA Modules:
  0.0 54.1 jit_solution(15829310129854609202)
XLA Ops:
  0.7 2.5 %pack.1 = bf16[128,5632]{1,0:T(8,128)(2,1)S(1)} custom-call(s32[1]{0:T(128)S(6)} %copy.6.counts_hbm, bf16[1,6,256,128]{3,2,1,0:T(8,128)(2,1)} %green_hbm.1, bf16[2,6,256,128]{3,2,1,0:T(8,128)(2,1)} %strain_hbm.1, s32[1,32]{1,0:T(1,128)} %events_hbm.1, f32[1,32,256]{2,1,0:T(8,128)} %resid_hbm.1), custom_call_target="tpu_custom_call" | custom-call | tf_op jit(solution)/shard_map/pack/pallas_call | solution.py:73
  3.1 46.4 %all_to_all.5.y_ref = bf16[16,8,5632]{2,1,0:T(8,128)(2,1)S(1)} all-to-all(bf16[16,8,5632]{2,1,0:T(8,128)(2,1)S(1)} %bitcast.2), channel_id=1, replica_groups=mesh['vox'=32,'sta'=16] {'sta'}, dimensions={0} | all-to-all | bytes 2883584 | tf_op jit(solution)/shard_map/all_to_all | solution.py:174
  49.5 4.6 %product.1 = f32[1,8]{1,0:T(1,128)} custom-call(bf16[16,8,5632]{2,1,0:T(8,128)(2,1)S(1)} %all_to_all.5.y_ref), custom_call_target="tpu_custom_call" | custom-call | tf_op jit(solution)/shard_map/product/pallas_call | solution.py:156

commit v3 on v2

--- a/solution.py
+++ b/solution.py
@@ -23,24 +23,19 @@
 
 def pack_kernel(
     counts_hbm, green_hbm, strain_hbm, events_hbm, resid_hbm, out_ref,
-    count_ref, green_ref, strain_ref, events_ref, resid_ref, small_sem, green_sem, strain_sem,
+    count_ref, green_ref, strain_ref, events_ref, resid_ref, small_sem, large_sem,
 ):
     small = [
         pltpu.make_async_copy(counts_hbm, count_ref, small_sem.at[0]),
         pltpu.make_async_copy(events_hbm, events_ref, small_sem.at[1]),
         pltpu.make_async_copy(resid_hbm, resid_ref, small_sem.at[2]),
     ]
-    greens = [
-        pltpu.make_async_copy(green_hbm.at[:, c], green_ref.at[:, c], green_sem.at[c]) for c in range(COMP)
-    ]
-    strains = [
-        pltpu.make_async_copy(strain_hbm.at[:, c], strain_ref.at[:, c], strain_sem.at[c]) for c in range(COMP)
-    ]
+    strain_copy = pltpu.make_async_copy(strain_hbm, strain_ref, large_sem.at[0])
+    green_copy = pltpu.make_async_copy(green_hbm, green_ref, large_sem.at[1])
     for copy in small:
         copy.start()
-    for c in range(COMP):
-        strains[c].start()
-        greens[c].start()
+    strain_copy.start()
+    green_copy.start()
     for copy in small:
         copy.wait()
     voxels = green_ref.shape[-1]
@@ -52,8 +47,8 @@
         match = (paired == 8 * m + row % 8) & (slot < count_ref[0])
         picked = jnp.dot(match.astype(F32).astype(BF16), wave, preferred_element_type=F32)
         out_ref[:, R_AT + m * NT : R_AT + (m + 1) * NT] = picked.astype(BF16)
+    strain_copy.wait()
     for c in range(COMP):
-        strains[c].wait()
         for half in range(2):
             rows = []
             for j in range(half * BLOCKS // 2, (half + 1) * BLOCKS // 2):
@@ -62,7 +57,8 @@
             block = jnp.concatenate(rows, axis=0)
             at = c * 2 * NT + half * NT
             out_ref[:, at : at + NT] = block.T
-        greens[c].wait()
+    green_copy.wait()
+    for c in range(COMP):
         at = G_AT + c * NT
         out_ref[:, at : at + NT] = green_ref[0, c].T
 
@@ -82,8 +78,7 @@
             pltpu.VMEM(events.shape, events.dtype),
             pltpu.VMEM(resid.shape, resid.dtype),
             pltpu.SemaphoreType.DMA((3,)),
-            pltpu.SemaphoreType.DMA((COMP,)),
-            pltpu.SemaphoreType.DMA((COMP,)),
+            pltpu.SemaphoreType.DMA((2,)),
         ],
         compiler_params=pltpu.CompilerParams(vmem_limit_bytes=48 << 20),
         name="pack",

time: 54.2 us -> 53.5 us (0.987)
  the two profiles are of different devices: /device:TPU:72 before, /device:TPU:200 now
where the time goes in v3:
time: 53.5 us; the launch traced here: 53.3 us
  blocking collectives  46.4 us (87%)
  Pallas kernels  6.26 us (12%)
  between operations  0.66 us (1%)
    all_to_all x1, blocking collectives, body(): lax.all_to_all(tiles, 'sta', split_axis=0, concat_axis=0, tiled=True)  46.4 us
    pallas_call x1, Pallas kernels, product(): pl.pallas_call(product_kernel, out_shape=jax.ShapeDtypeStruct((1, OWN), F...  4.55 us
    pallas_call x1, Pallas kernels, pack(): pl.pallas_call(pack_kernel, out_shape=jax.ShapeDtypeStruct((voxels, COLS)...  1.71 us

profile of v3, /device:TPU:200, one launch (start us, length us, event | category | flops | bytes accessed | tf_op | source)
XLA Modules:
  0.0 53.3 jit_solution(1738783135686648596)
XLA Ops:
  0.7 1.7 %pack.1 = bf16[128,5632]{1,0:T(8,128)(2,1)S(1)} custom-call(s32[1]{0:T(128)S(6)} %copy.6.counts_hbm, bf16[1,6,256,128]{3,2,1,0:T(8,128)(2,1)} %green_hbm.1, bf16[2,6,256,128]{3,2,1,0:T(8,128)(2,1)} %strain_hbm.1, s32[1,32]{1,0:T(1,128)} %events_hbm.1, f32[1,32,256]{2,1,0:T(8,128)} %resid_hbm.1), custom_call_target="tpu_custom_call" | custom-call | tf_op jit(solution)/shard_map/pack/pallas_call | solution.py:69
  2.4 46.4 %all_to_all.5.y_ref = bf16[16,8,5632]{2,1,0:T(8,128)(2,1)S(1)} all-to-all(bf16[16,8,5632]{2,1,0:T(8,128)(2,1)S(1)} %bitcast.2), channel_id=1, replica_groups=mesh['vox'=32,'sta'=16] {'sta'}, dimensions={0} | all-to-all | bytes 2883584 | tf_op jit(solution)/shard_map/all_to_all | solution.py:169
  48.8 4.6 %product.1 = f32[1,8]{1,0:T(1,128)} custom-call(bf16[16,8,5632]{2,1,0:T(8,128)(2,1)S(1)} %all_to_all.5.y_ref), custom_call_target="tpu_custom_call" | custom-call | tf_op jit(solution)/shard_map/product/pallas_call | solution.py:151

commit v4 on v3

--- a/solution.py
+++ b/solution.py
@@ -17,6 +17,7 @@
 G_AT = S_COLS
 R_AT = G_AT + COMP * NT
 COLS = R_AT + (EVENTS // 8) * NT
+ORDER = (12, 4, 5, 0, 9, 3, 1, 10, 7, 14, 2, 11, 6, 15, 13, 8)
 F32 = jnp.float32
 BF16 = jnp.bfloat16
 
@@ -39,6 +40,11 @@
     for copy in small:
         copy.wait()
     voxels = green_ref.shape[-1]
+
+    def put(at, rows):
+        for i, member in enumerate(ORDER):
+            out_ref[i, :, at : at + NT] = rows[member * OWN : (member + 1) * OWN].astype(BF16)
+
     wave = resid_ref[0].astype(BF16)
     row = lax.broadcasted_iota(jnp.int32, (voxels, MAXP), 0)
     slot = lax.broadcasted_iota(jnp.int32, (voxels, MAXP), 1)
@@ -46,7 +52,7 @@
     for m in range(EVENTS // 8):
         match = (paired == 8 * m + row % 8) & (slot < count_ref[0])
         picked = jnp.dot(match.astype(F32).astype(BF16), wave, preferred_element_type=F32)
-        out_ref[:, R_AT + m * NT : R_AT + (m + 1) * NT] = picked.astype(BF16)
+        put(R_AT + m * NT, picked)
     strain_copy.wait()
     for c in range(COMP):
         for half in range(2):
@@ -56,19 +62,18 @@
                     rows.append(strain_ref[e, c, LAG * j : LAG * (j + 1), :])
             block = jnp.concatenate(rows, axis=0)
             at = c * 2 * NT + half * NT
-            out_ref[:, at : at + NT] = block.T
+            put(at, block.T)
     green_copy.wait()
     for c in range(COMP):
         at = G_AT + c * NT
-        out_ref[:, at : at + NT] = green_ref[0, c].T
+        put(at, green_ref[0, c].T)
 
 
 def pack(green, strain, events, counts, resid):
-    voxels = green.shape[-1]
     whole = pl.BlockSpec(memory_space=pltpu.HBM)
     return pl.pallas_call(
         pack_kernel,
-        out_shape=jax.ShapeDtypeStruct((voxels, COLS), BF16),
+        out_shape=jax.ShapeDtypeStruct((STA, OWN, COLS), BF16),
         in_specs=[whole] * 5,
         out_specs=pl.BlockSpec(memory_space=pltpu.VMEM),
         scratch_shapes=[
@@ -112,7 +117,8 @@
             for q in range(8):
                 wave = jnp.broadcast_to(waves[q : q + 1, :], (LAG, NT))
                 shifted = pltpu.roll(wave, 0, 1, stride=1, stride_axis=0)
-                at = (8 * m + q) * LAG
+                e = 8 * m + q
+                at = (2 * ORDER.index(e // 2) + e % 2) * LAG
                 w_ref[at : at + LAG, :] = jnp.where(upper, shifted, 0.0).astype(BF16)
 
     def station(s, w_ref, total):
@@ -165,8 +171,9 @@
 
 def body(green_tensor, strain, pair_events, pair_counts, residuals):
     packed = pack(green_tensor, strain, pair_events, pair_counts, residuals)
-    tiles = packed.reshape(STA, OWN, COLS)
-    arrived = lax.all_to_all(tiles, "sta", split_axis=0, concat_axis=0, tiled=True)
+    arrived = lax.all_to_all(
+        packed, "sta", split_axis=0, concat_axis=0, tiled=True, axis_index_groups=[list(ORDER)]
+    )
     return product(arrived).reshape(OWN)
 
 

time: 53.5 us -> 50 us (0.935)
  the two profiles are of different devices: /device:TPU:200 before, /device:TPU:6 now
where the time goes in v4:
time: 50 us; the launch traced here: 49.4 us
  blocking collectives  42.4 us (85%)
  Pallas kernels  6.38 us (13%)
  between operations  0.66 us (1%)
    all_to_all x1, blocking collectives, body(): lax.all_to_all(packed, 'sta', split_axis=0, concat_axis=0, tiled=True, ax...  42.4 us
    pallas_call x1, Pallas kernels, product(): pl.pallas_call(product_kernel, out_shape=jax.ShapeDtypeStruct((1, OWN), F...  4.67 us
    pallas_call x1, Pallas kernels, pack(): pl.pallas_call(pack_kernel, out_shape=jax.ShapeDtypeStruct((STA, OWN, COL...  1.71 us

profile of v4, /device:TPU:6, one launch (start us, length us, event | category | flops | bytes accessed | tf_op | source)
XLA Modules:
  0.0 49.4 jit_solution(7463879618606038027)
XLA Ops:
  0.7 1.7 %pack.1 = bf16[16,8,5632]{2,1,0:T(8,128)(2,1)S(1)} custom-call(s32[1]{0:T(128)S(6)} %copy.6.counts_hbm, bf16[1,6,256,128]{3,2,1,0:T(8,128)(2,1)} %green_hbm.1, bf16[2,6,256,128]{3,2,1,0:T(8,128)(2,1)} %strain_hbm.1, s32[1,32]{1,0:T(1,128)} %events_hbm.1, f32[1,32,256]{2,1,0:T(8,128)} %resid_hbm.1), custom_call_target="tpu_custom_call" | custom-call | tf_op jit(solution)/shard_map/pack/pallas_call | solution.py:74
  2.4 42.4 %all_to_all.5.y_ref = bf16[16,8,5632]{2,1,0:T(8,128)(2,1)S(1)} all-to-all(bf16[16,8,5632]{2,1,0:T(8,128)(2,1)S(1)} %pack.1), channel_id=1, replica_groups={{12,4,5,0,9,3,1,10,7,14,2,11,6,15,13,8},{28,20,21,16,25,19,17,26,23,30,..., dimensions={0} | all-to-all | bytes 2883584 | tf_op jit(solution)/shard_map/all_to_all | solution.py:174
  44.8 4.7 %product.1 = f32[1,8]{1,0:T(1,128)} custom-call(bf16[16,8,5632]{2,1,0:T(8,128)(2,1)S(1)} %all_to_all.5.y_ref), custom_call_target="tpu_custom_call" | custom-call | tf_op jit(solution)/shard_map/product/pallas_call | solution.py:157

commit v5 on v4

--- a/solution.py
+++ b/solution.py
@@ -17,7 +17,7 @@
 G_AT = S_COLS
 R_AT = G_AT + COMP * NT
 COLS = R_AT + (EVENTS // 8) * NT
-ORDER = (12, 4, 5, 0, 9, 3, 1, 10, 7, 14, 2, 11, 6, 15, 13, 8)
+ORDER = (12, 14, 6, 7, 2, 8, 5, 13, 1, 0, 11, 15, 4, 3, 9, 10)
 F32 = jnp.float32
 BF16 = jnp.bfloat16
 
@@ -35,8 +35,8 @@
     green_copy = pltpu.make_async_copy(green_hbm, green_ref, large_sem.at[1])
     for copy in small:
         copy.start()
+    green_copy.start()
     strain_copy.start()
-    green_copy.start()
     for copy in small:
         copy.wait()
     voxels = green_ref.shape[-1]
@@ -53,6 +53,10 @@
         match = (paired == 8 * m + row % 8) & (slot < count_ref[0])
         picked = jnp.dot(match.astype(F32).astype(BF16), wave, preferred_element_type=F32)
         put(R_AT + m * NT, picked)
+    green_copy.wait()
+    for c in range(COMP):
+        at = G_AT + c * NT
+        put(at, green_ref[0, c].T)
     strain_copy.wait()
     for c in range(COMP):
         for half in range(2):
@@ -63,10 +67,6 @@
             block = jnp.concatenate(rows, axis=0)
             at = c * 2 * NT + half * NT
             put(at, block.T)
-    green_copy.wait()
-    for c in range(COMP):
-        at = G_AT + c * NT
-        put(at, green_ref[0, c].T)
 
 
 def pack(green, strain, events, counts, resid):

time: 50 us -> 49.8 us (level)
  no operation moved by 1% of the time
where the time goes in v5:
time: 49.8 us; the launch traced here: 49.3 us
  blocking collectives  42.4 us (85%)
  Pallas kernels  6.28 us (13%)
  between operations  0.66 us (1%)
    all_to_all x1, blocking collectives, body(): lax.all_to_all(packed, 'sta', split_axis=0, concat_axis=0, tiled=True, ax...  42.4 us
    pallas_call x1, Pallas kernels, product(): pl.pallas_call(product_kernel, out_shape=jax.ShapeDtypeStruct((1, OWN), F...  4.69 us
    pallas_call x1, Pallas kernels, pack(): pl.pallas_call(pack_kernel, out_shape=jax.ShapeDtypeStruct((STA, OWN, COL...  1.59 us

profile of v5, /device:TPU:6, one launch (start us, length us, event | category | flops | bytes accessed | tf_op | source)
XLA Modules:
  0.0 49.3 jit_solution(15269494621625151611)
XLA Ops:
  0.7 1.6 %pack.1 = bf16[16,8,5632]{2,1,0:T(8,128)(2,1)S(1)} custom-call(s32[1]{0:T(128)S(6)} %copy.6.counts_hbm, bf16[1,6,256,128]{3,2,1,0:T(8,128)(2,1)} %green_hbm.1, bf16[2,6,256,128]{3,2,1,0:T(8,128)(2,1)} %strain_hbm.1, s32[1,32]{1,0:T(1,128)} %events_hbm.1, f32[1,32,256]{2,1,0:T(8,128)} %resid_hbm.1), custom_call_target="tpu_custom_call" | custom-call | tf_op jit(solution)/shard_map/pack/pallas_call | solution.py:74
  2.2 42.4 %all_to_all.5.y_ref = bf16[16,8,5632]{2,1,0:T(8,128)(2,1)S(1)} all-to-all(bf16[16,8,5632]{2,1,0:T(8,128)(2,1)S(1)} %pack.1), channel_id=1, replica_groups={{12,14,6,7,2,8,5,13,1,0,11,15,4,3,9,10},{28,30,22,23,18,24,21,29,17,16,..., dimensions={0} | all-to-all | bytes 2883584 | tf_op jit(solution)/shard_map/all_to_all | solution.py:174
  44.7 4.7 %product.1 = f32[1,8]{1,0:T(1,128)} custom-call(bf16[16,8,5632]{2,1,0:T(8,128)(2,1)S(1)} %all_to_all.5.y_ref), custom_call_target="tpu_custom_call" | custom-call | tf_op jit(solution)/shard_map/product/pallas_call | solution.py:157

commit v6 on v5

--- a/solution.py
+++ b/solution.py
@@ -17,7 +17,7 @@
 G_AT = S_COLS
 R_AT = G_AT + COMP * NT
 COLS = R_AT + (EVENTS // 8) * NT
-ORDER = (12, 14, 6, 7, 2, 8, 5, 13, 1, 0, 11, 15, 4, 3, 9, 10)
+ORDER = (13, 6, 12, 8, 10, 0, 14, 9, 7, 15, 2, 4, 3, 5, 11, 1)
 F32 = jnp.float32
 BF16 = jnp.bfloat16
 

time: 49.8 us -> 49.6 us (level)
  no operation moved by 1% of the time
where the time goes in v6:
time: 49.6 us; the launch traced here: 49.4 us
  blocking collectives  42.5 us (86%)
  Pallas kernels  6.27 us (13%)
  between operations  0.66 us (1%)
    all_to_all x1, blocking collectives, body(): lax.all_to_all(packed, 'sta', split_axis=0, concat_axis=0, tiled=True, ax...  42.5 us
    pallas_call x1, Pallas kernels, product(): pl.pallas_call(product_kernel, out_shape=jax.ShapeDtypeStruct((1, OWN), F...  4.68 us
    pallas_call x1, Pallas kernels, pack(): pl.pallas_call(pack_kernel, out_shape=jax.ShapeDtypeStruct((STA, OWN, COL...  1.59 us

profile of v6, /device:TPU:6, one launch (start us, length us, event | category | flops | bytes accessed | tf_op | source)
XLA Modules:
  0.0 49.4 jit_solution(11516346379870003657)
XLA Ops:
  0.7 1.6 %pack.1 = bf16[16,8,5632]{2,1,0:T(8,128)(2,1)S(1)} custom-call(s32[1]{0:T(128)S(6)} %copy.6.counts_hbm, bf16[1,6,256,128]{3,2,1,0:T(8,128)(2,1)} %green_hbm.1, bf16[2,6,256,128]{3,2,1,0:T(8,128)(2,1)} %strain_hbm.1, s32[1,32]{1,0:T(1,128)} %events_hbm.1, f32[1,32,256]{2,1,0:T(8,128)} %resid_hbm.1), custom_call_target="tpu_custom_call" | custom-call | tf_op jit(solution)/shard_map/pack/pallas_call | solution.py:74
  2.2 42.5 %all_to_all.5.y_ref = bf16[16,8,5632]{2,1,0:T(8,128)(2,1)S(1)} all-to-all(bf16[16,8,5632]{2,1,0:T(8,128)(2,1)S(1)} %pack.1), channel_id=1, replica_groups={{13,6,12,8,10,0,14,9,7,15,2,4,3,5,11,1},{29,22,28,24,26,16,30,25,23,31,..., dimensions={0} | all-to-all | bytes 2883584 | tf_op jit(solution)/shard_map/all_to_all | solution.py:174
  44.8 4.7 %product.1 = f32[1,8]{1,0:T(1,128)} custom-call(bf16[16,8,5632]{2,1,0:T(8,128)(2,1)S(1)} %all_to_all.5.y_ref), custom_call_target="tpu_custom_call" | custom-call | tf_op jit(solution)/shard_map/product/pallas_call | solution.py:157

commit v7 on v6

--- a/solution.py
+++ b/solution.py
@@ -31,12 +31,15 @@
         pltpu.make_async_copy(events_hbm, events_ref, small_sem.at[1]),
         pltpu.make_async_copy(resid_hbm, resid_ref, small_sem.at[2]),
     ]
-    strain_copy = pltpu.make_async_copy(strain_hbm, strain_ref, large_sem.at[0])
+    strain_copies = [
+        pltpu.make_async_copy(strain_hbm.at[e], strain_ref.at[e], large_sem.at[2 * e]) for e in range(2)
+    ]
     green_copy = pltpu.make_async_copy(green_hbm, green_ref, large_sem.at[1])
     for copy in small:
         copy.start()
     green_copy.start()
-    strain_copy.start()
+    for copy in strain_copies:
+        copy.start()
     for copy in small:
         copy.wait()
     voxels = green_ref.shape[-1]
@@ -57,7 +60,8 @@
     for c in range(COMP):
         at = G_AT + c * NT
         put(at, green_ref[0, c].T)
-    strain_copy.wait()
+    for copy in strain_copies:
+        copy.wait()
     for c in range(COMP):
         for half in range(2):
             rows = []
@@ -83,7 +87,7 @@
             pltpu.VMEM(events.shape, events.dtype),
             pltpu.VMEM(resid.shape, resid.dtype),
             pltpu.SemaphoreType.DMA((3,)),
-            pltpu.SemaphoreType.DMA((2,)),
+            pltpu.SemaphoreType.DMA((3,)),
         ],
         compiler_params=pltpu.CompilerParams(vmem_limit_bytes=48 << 20),
         name="pack",

time: 49.6 us -> 49.7 us (level)
  no operation moved by 1% of the time
where the time goes in v7:
time: 49.7 us; the launch traced here: 49.5 us
  blocking collectives  42.5 us (86%)
  Pallas kernels  6.36 us (13%)
  between operations  0.66 us (1%)
    all_to_all x1, blocking collectives, body(): lax.all_to_all(packed, 'sta', split_axis=0, concat_axis=0, tiled=True, ax...  42.5 us
    pallas_call x1, Pallas kernels, product(): pl.pallas_call(product_kernel, out_shape=jax.ShapeDtypeStruct((1, OWN), F...  4.68 us
    pallas_call x1, Pallas kernels, pack(): pl.pallas_call(pack_kernel, out_shape=jax.ShapeDtypeStruct((STA, OWN, COL...  1.68 us

profile of v7, /device:TPU:6, one launch (start us, length us, event | category | flops | bytes accessed | tf_op | source)
XLA Modules:
  0.0 49.5 jit_solution(1924085950994752121)
XLA Ops:
  0.7 1.7 %pack.1 = bf16[16,8,5632]{2,1,0:T(8,128)(2,1)S(1)} custom-call(s32[1]{0:T(128)S(6)} %copy.6.counts_hbm, bf16[1,6,256,128]{3,2,1,0:T(8,128)(2,1)} %green_hbm.1, bf16[2,6,256,128]{3,2,1,0:T(8,128)(2,1)} %strain_hbm.1, s32[1,32]{1,0:T(1,128)} %events_hbm.1, f32[1,32,256]{2,1,0:T(8,128)} %resid_hbm.1), custom_call_target="tpu_custom_call" | custom-call | tf_op jit(solution)/shard_map/pack/pallas_call | solution.py:78
  2.3 42.5 %all_to_all.5.y_ref = bf16[16,8,5632]{2,1,0:T(8,128)(2,1)S(1)} all-to-all(bf16[16,8,5632]{2,1,0:T(8,128)(2,1)S(1)} %pack.1), channel_id=1, replica_groups={{13,6,12,8,10,0,14,9,7,15,2,4,3,5,11,1},{29,22,28,24,26,16,30,25,23,31,..., dimensions={0} | all-to-all | bytes 2883584 | tf_op jit(solution)/shard_map/all_to_all | solution.py:178
  44.8 4.7 %product.1 = f32[1,8]{1,0:T(1,128)} custom-call(bf16[16,8,5632]{2,1,0:T(8,128)(2,1)S(1)} %all_to_all.5.y_ref), custom_call_target="tpu_custom_call" | custom-call | tf_op jit(solution)/shard_map/product/pallas_call | solution.py:161
